TPU v7x, 32 devices: a whole 2x2x4 slice. The times are simulated.
32 devices in a mesh: leaf: 8 (over z, y), row: 2 (over core), col: 2 (over x).
Axes of the slice: x: 2, y: 2, z: 4, core: 2. Of those that a mesh axis runs over, the one named last changes fastest.
Arguments:
- sigma_top: float32 [4096, 4096], P('row', ('leaf', 'col'))
- structure: int32 [8, 16], replicated, may hold values from 0 to 31, as said below
- lower: float32 [8, 2048, 2048], P('leaf', 'row', 'col'), may hold values from -0.25 to 0.25
- dinv: float32 [8, 2048, 2048], P('leaf', 'row', 'col'), may hold values from -6 to 6
Outputs:
- sigma_sj: float32 [8, 2048, 2048], P('leaf', 'row', 'col')
- sigma_jj: float32 [8, 2048, 2048], P('leaf', 'row', 'col')
Inputs may be any that keep to these rules, and one draw needn't show every extreme that they name: `structure`: each row lists 16 distinct tiles in increasing order and always holds tile 0 and tile 32 - 1.
All inputs are finite; a program needn't handle non-finite values.
Results may differ from a plain program's by a relative error of at most 0.0003.
Values sent between devices are 32-bit elements; how exact they have to be, the bound alone decides.
No kernel may reach another device: no remote copies, remote signals or barrier semaphores. Data moves between devices by JAX's collectives and lax.ppermute only.
A program may use at most 192 MiB of HBM per device.

v0:
```python
import jax
import jax.numpy as jnp
from jax import lax
from jax.sharding import PartitionSpec as P

TILE = 128


def body(sigma_top, structure, lower, dinv):
    factor_block = lower[0]
    diag_inverse = dinv[0]
    struct_rows = factor_block.shape[0]
    n_row = lax.axis_size("row")
    n_col = lax.axis_size("col")
    total_rows = struct_rows * n_row
    root_rows = sigma_top.shape[0]
    within = jnp.arange(TILE, dtype=jnp.int32)
    all_indices = (structure[:, :, None] * TILE + within[None, None, :]).reshape(
        structure.shape[0], -1
    )
    leaf_index = lax.axis_index("leaf")
    own_indices = lax.dynamic_index_in_dim(all_indices, leaf_index, 0, keepdims=False)
    first_root_row = lax.axis_index("row") * root_rows
    quarter = total_rows // n_col
    wanted_cols = lax.dynamic_slice_in_dim(own_indices, lax.axis_index("col") * quarter, quarter)
    empty_cols = jnp.zeros((root_rows, quarter), jnp.float32)
    shard_piece = lax.all_gather(sigma_top, ("leaf", "col"), axis=1, tiled=True)
    piece_width = shard_piece.shape[1]
    inside = (wanted_cols >= 0) & (wanted_cols < piece_width)
    values = jnp.take(shard_piece, jnp.clip(wanted_cols, 0, piece_width - 1), axis=1)
    picked_cols = jnp.where(inside[None, :], values, empty_cols)
    wanted = own_indices - first_root_row
    inside = (wanted >= 0) & (wanted < root_rows)
    values = jnp.take(picked_cols, jnp.clip(wanted, 0, root_rows - 1), axis=0)
    sigma_block = lax.psum_scatter(
        jnp.where(inside[:, None], values, 0.0), "row", scatter_dimension=0, tiled=True
    )
    row_panel = lax.all_gather(sigma_block, "col", axis=1, tiled=True)
    cross = -jnp.dot(
        row_panel,
        lax.all_gather(factor_block, "row", axis=0, tiled=True),
        precision=lax.Precision.HIGHEST,
        preferred_element_type=jnp.float32,
    )
    factor_rows = lax.all_gather(factor_block, "col", axis=1, tiled=True)
    front = diag_inverse + lax.psum_scatter(
        -lax.dot_general(
            factor_rows,
            cross,
            (((0,), (0,)), ((), ())),
            precision=lax.Precision.HIGHEST,
            preferred_element_type=jnp.float32,
        ),
        "row",
        scatter_dimension=0,
        tiled=True,
    )
    return (cross[None], front[None])


def solution(mesh):
    placed = (P("row", ("leaf", "col")), P(), P("leaf", "row", "col"), P("leaf", "row", "col"))
    return jax.shard_map(
        body,
        mesh=mesh,
        in_specs=placed,
        out_specs=(P("leaf", "row", "col"), P("leaf", "row", "col")),
        check_vma=False,
    )
```

profile of v0, /device:TPU:0, one launch (start us, length us, event | category | flops | bytes accessed | tf_op | source)
XLA Modules:
  0.0 738.3 jit_solution(9349008275643625200)
XLA Ops:
  7.2 0.0 all-gather.7.cloned.1.call-start
  7.2 2.9 copy.11
  10.1 0.0 all-gather.7.cloned.1.call-update
  10.1 0.0 reduce-scatter.3.cloned.1.call-start
  10.2 0.7 broadcast_multiply_fusion
  10.9 0.1 copy.10
  10.9 0.1 bitcast_add_fusion.1
  11.0 0.1 and_reduce_fusion.1
  11.1 0.1 and_reduce_fusion
  11.2 0.1 compare_select_fusion.1
  11.4 353.6 %all-gather.7.cloned.1.call-done = f32[2048,4096]{0,1:T(8,128)} async-done(((f32[2048,256]{0,1:T(8,128)}), f32[2048,4096]{0,1:T(8,128)}) %all-gather.7.cloned.1.call-update) | async-done | bytes 33554448 | tf_op jit(solution)/shard_map/all_gather | solution.py:27
  364.9 19.6 %gather_fusion = f32[1024,2048]{1,0:T(8,128)} fusion(f32[2048,4096]{0,1:T(8,128)} %all-gather.7.cloned.1.call-done, s32[1024]{0:T(1024)S(1)} %broadcast_clamp_fusion.2), kind=kCustom, calls=%fused_computation | custom fusion | bytes 16781312 | tf_op jit(solution)/shard_map/jit(_take)/gather | solution.py:30
  384.5 6.2 select_bitcast_fusion
  390.7 9.3 %copy.12 = f32[2048,1024]{1,0:T(8,128)} copy(f32[2048,1024]{0,1:T(8,128)} %select_bitcast_fusion) | data formatting | bytes 16777216 | tf_op jit(solution)/shard_map/jit(_where)/select_n | solution.py:31
  400.0 15.1 %gather_fusion.1 = f32[2048,1024]{1,0:T(8,128)} fusion(f32[2048,1024]{1,0:T(8,128)} %copy.12, s32[2048]{0:T(1024)S(1)} %broadcast_clamp_fusion), kind=kCustom, calls=%fused_computation.1 | custom fusion | bytes 16785408 | tf_op jit(solution)/shard_map/jit(_take)/gather | solution.py:34
  415.1 5.9 select_select_fusion
  421.0 0.0 reduce-scatter.3.cloned.1.call-update
  421.1 0.0 all-gather.11.cloned.1.call-start
  421.1 0.7 all-gather.11.cloned.1.call-update
  421.8 0.0 all-gather.9.cloned.1.call-start
  421.9 14.4 %reduce-scatter.3.cloned.1.call-done = f32[1024,1024]{1,0:T(8,128)} async-done(((f32[2048,1024]{1,0:T(8,128)}), f32[1024,1024]{1,0:T(8,128)}) %reduce-scatter.3.cloned.1.call-update) | async-done | bytes 4194320 | tf_op jit(solution)/shard_map/reduce_scatter | solution.py:35
  436.2 0.0 all-gather.9.cloned.1.call-update
  436.2 0.0 all-gather.13.cloned.1.call-start
  436.3 0.5 all-gather.13.cloned.1.call-update
  436.8 0.0 reduce-scatter.5.cloned.1.call-start
  436.9 22.1 %all-gather.11.cloned.1.call-done = f32[1,2048,1024]{2,1,0:T(8,128)} async-done(((f32[1,1024,1024]{2,1,0:T(8,128)}), f32[1,2048,1024]{2,1,0:T(8,128)}) %all-gather.11.cloned.1.call-update) | async-done | bytes 8388624 | tf_op jit(solution)/shard_map/all_gather | solution.py:41
  459.0 106.7 %all-gather.9.cloned.1.call-done = f32[1024,2048]{1,0:T(8,128)} async-done(((f32[1024,1024]{1,0:T(8,128)}), f32[1024,2048]{1,0:T(8,128)}) %all-gather.9.cloned.1.call-update) | async-done | bytes 8388624 | tf_op jit(solution)/shard_map/all_gather | solution.py:38
  565.7 31.8 %fusion.2 = f32[1024,1024]{1,0:T(8,128)} fusion(f32[1024,2048]{1,0:T(8,128)} %all-gather.9.cloned.1.call-done, f32[1,2048,1024]{2,1,0:T(8,128)} %all-gather.11.cloned.1.call-done), kind=kOutput, calls=%fused_computation.4 | convolution fusion | flops 25769803776 | bytes 20971520 | tf_op jit(solution)/shard_map/dot_general | solution.py:39
  597.5 73.7 %all-gather.13.cloned.1.call-done = f32[1,1024,2048]{2,1,0:T(8,128)} async-done(((f32[1,1024,1024]{2,1,0:T(8,128)}), f32[1,1024,2048]{2,1,0:T(8,128)}) %all-gather.13.cloned.1.call-update) | async-done | bytes 8388624 | tf_op jit(solution)/shard_map/all_gather | solution.py:45
  671.2 31.2 %negate_bitcast_fusion = f32[2048,1024]{0,1:T(8,128)} fusion(f32[1,1024,2048]{2,1,0:T(8,128)} %all-gather.13.cloned.1.call-done, f32[1024,1024]{1,0:T(8,128)} %fusion.2), kind=kOutput, calls=%fused_computation.7 | convolution fusion | flops 25772949504 | bytes 20971520 | tf_op jit(solution)/shard_map/dot_general | solution.py:47
  702.3 0.0 reduce-scatter.5.cloned.1.call-update
  702.4 5.4 copy.13
  707.7 6.1 negate_bitcast_fusion.1
  713.8 5.5 reduce-scatter.5.cloned.1.call-done
  719.3 6.8 fusion.6
  726.1 5.3 copy.14
  (6 shorter events, 0.1 us)
Async XLA Ops:
  7.2 357.8 %all-gather.7.cloned.1.call-start = ((), (), s32[]{:S(2)}) async-start(), calls=%async_computation.2 | async-start | bytes 35651584 | tf_op jit(solution)/shard_map/all_gather | solution.py:27
  10.1 426.1 %reduce-scatter.3.cloned.1.call-start = ((), (), s32[]{:S(2)}) async-start(), calls=%async_computation.3 | async-start | bytes 12582912 | tf_op jit(solution)/shard_map/reduce_scatter | solution.py:35
  421.1 37.9 %all-gather.11.cloned.1.call-start = ((), (), s32[]{:S(2)}) async-start(), calls=%async_computation.6 | async-start | bytes 12582912 | tf_op jit(solution)/shard_map/all_gather | solution.py:41
  421.8 143.9 %all-gather.9.cloned.1.call-start = ((), (), s32[]{:S(2)}) async-start(), calls=%async_computation.4 | async-start | bytes 12582912 | tf_op jit(solution)/shard_map/all_gather | solution.py:38
  436.2 234.9 %all-gather.13.cloned.1.call-start = ((), (), s32[]{:S(2)}) async-start(), calls=%async_computation.7 | async-start | bytes 12582912 | tf_op jit(solution)/shard_map/all_gather | solution.py:45
  436.8 282.5 %reduce-scatter.5.cloned.1.call-start = ((), (), s32[]{:S(2)}) async-start(), calls=%async_computation.5 | async-start | bytes 12582912 | tf_op jit(solution)/shard_map/reduce_scatter | solution.py:46
Sparse Core Ops, SparseCore 0:
  11.3 353.5 all-gather.6
  421.2 14.9 reduce-scatter.2
  437.8 21.1 all-gather.10
  460.5 105.1 all-gather.8
  567.1 103.9 all-gather.12
  702.5 16.7 reduce-scatter.4
where the time goes:
time: 739 us; the launch traced here: 738 us
  waiting for transfers between devices  577 us (78%)
  matrix products  63 us (9%)
  local copies, waits for them, and re-layouts  57.6 us (8%)
  other arithmetic  26.1 us (4%)
  between operations  14.2 us (2%)
    all_gather x1, waiting for transfers between devices, body(): shard_piece = lax.all_gather(sigma_top, ('leaf', 'col'), axis=1, tiled=True)  354 us
    all_gather x1, waiting for transfers between devices, body(): row_panel = lax.all_gather(sigma_block, 'col', axis=1, tiled=True)  107 us
    all_gather x1, waiting for transfers between devices, body(): factor_rows = lax.all_gather(factor_block, 'col', axis=1, tiled=True)  73.7 us
    dot_general x1, matrix products, body(): jnp.dot(row_panel, lax.all_gather(factor_block, 'row', axis=0, tiled=True...  31.8 us
    dot_general x1, matrix products, body(): lax.dot_general(factor_rows, cross, (((0,), (0,)), ((), ())), precision=l...  31.2 us
    all_gather x1, waiting for transfers between devices, body(): lax.all_gather(factor_block, 'row', axis=0, tiled=True)  22.1 us
    gather x1, local copies, waits for them, and re-layouts, body(): jnp.take(shard_piece, jnp.clip(wanted_cols, 0, piece_width - 1), axis=1)  19.6 us
    gather x1, local copies, waits for them, and re-layouts, body(): values = jnp.take(picked_cols, jnp.clip(wanted, 0, root_rows - 1), axis=0)  15.1 us
  transfers between devices with their start and end apart: 6, of which 6 were waited for; matrix products, arithmetic and copies ran while one was open for 6% of the time, Pallas kernels for 0%

commit v1 on v0

--- a/solution.py
+++ b/solution.py
@@ -42,7 +42,14 @@
         precision=lax.Precision.HIGHEST,
         preferred_element_type=jnp.float32,
     )
-    factor_rows = lax.all_gather(factor_block, "col", axis=1, tiled=True)
+    ways, here = (lax.axis_size("col"), lax.axis_index("col"))
+    factor_rows, reach = (factor_block, 1)
+    while reach < ways:
+        theirs = lax.ppermute(factor_rows, "col", [(d, d ^ reach) for d in range(ways)])
+        mine_first = jnp.concatenate([factor_rows, theirs], axis=1)
+        theirs_first = jnp.concatenate([theirs, factor_rows], axis=1)
+        factor_rows = jnp.where(here & reach == 0, mine_first, theirs_first)
+        reach = 2 * reach
     front = diag_inverse + lax.psum_scatter(
         -lax.dot_general(
             factor_rows,

time: 739 us -> 714 us (0.966)
  waiting for transfers between devices: 577 us -> 563 us
  local copies, waits for them, and re-layouts: 57.6 us -> 48.9 us
    all_gather x1 -> x0, waiting for transfers between devices: 73.7 us -> none  [body(): factor_rows = lax.all_gather(factor_block, 'col', axis=1, tiled=True)]
    all_gather x1, waiting for transfers between devices: 107 us -> 160 us  [body(): row_panel = lax.all_gather(sigma_block, 'col', axis=1, tiled=True)]
    unnamed x3 -> x5, local copies, waits for them, and re-layouts: 13.6 us -> 4.89 us
    reduce_scatter x1, waiting for transfers between devices: 5.49 us -> 13.1 us  [body(): lax.psum_scatter(-lax.dot_general(factor_rows, cross, (((0,), (0,)), ((),...]
  transfers between devices with their start and end apart: 6 -> 6, of which waited for: 6 -> 5; matrix products, arithmetic and copies ran while one was open for 6% -> 5% of each run, Pallas kernels for 0% -> 0%
where the time goes in v1:
time: 714 us
  waiting for transfers between devices  563 us (79%)
  matrix products  60.9 us (9%)
  local copies, waits for them, and re-layouts  48.9 us (7%)
  other arithmetic  25.1 us (4%)
  between operations  13.9 us (2%)
    all_gather x1, waiting for transfers between devices, body(): shard_piece = lax.all_gather(sigma_top, ('leaf', 'col'), axis=1, tiled=True)  354 us
    all_gather x1, waiting for transfers between devices, body(): row_panel = lax.all_gather(sigma_block, 'col', axis=1, tiled=True)  160 us
    dot_general x1, matrix products, body(): lax.dot_general(factor_rows, cross, (((0,), (0,)), ((), ())), precision=l...  31 us
    dot_general x1, matrix products, body(): jnp.dot(row_panel, lax.all_gather(factor_block, 'row', axis=0, tiled=True...  29.9 us
    all_gather x1, waiting for transfers between devices, body(): lax.all_gather(factor_block, 'row', axis=0, tiled=True)  20.8 us
    gather x1, local copies, waits for them, and re-layouts, body(): jnp.take(shard_piece, jnp.clip(wanted_cols, 0, piece_width - 1), axis=1)  19.6 us
    gather x1, local copies, waits for them, and re-layouts, body(): values = jnp.take(picked_cols, jnp.clip(wanted, 0, root_rows - 1), axis=0)  15.1 us
    reduce_scatter x1, waiting for transfers between devices, body(): lax.psum_scatter(jnp.where(inside[:, None], values, 0.0), 'row', scatter_...  14.4 us
  transfers between devices with their start and end apart: 6, of which 5 were waited for; matrix products, arithmetic and copies ran while one was open for 5% of the time, Pallas kernels for 0%

profile of v1, /device:TPU:0, one launch (start us, length us, event | category | flops | bytes accessed | tf_op | source)
XLA Modules:
  0.0 714.0 jit_solution(5489871801818853892)
XLA Ops:
  7.2 0.0 all-gather.5.cloned.1.call-start
  7.2 2.9 copy.9
  10.1 0.0 all-gather.5.cloned.1.call-update
  10.1 0.0 reduce-scatter.3.cloned.1.call-start
  10.2 0.7 broadcast_multiply_fusion
  10.9 0.1 copy.8
  11.0 0.1 bitcast_add_fusion.1
  11.0 0.1 and_reduce_fusion.1
  11.1 0.1 and_reduce_fusion
  11.2 0.1 compare_select_fusion.1
  11.4 353.6 %all-gather.5.cloned.1.call-done = f32[2048,4096]{0,1:T(8,128)} async-done(((f32[2048,256]{0,1:T(8,128)}), f32[2048,4096]{0,1:T(8,128)}) %all-gather.5.cloned.1.call-update) | async-done | bytes 33554448 | tf_op jit(solution)/shard_map/all_gather | solution.py:27
  364.9 19.6 %gather_fusion = f32[1024,2048]{1,0:T(8,128)} fusion(f32[2048,4096]{0,1:T(8,128)} %all-gather.5.cloned.1.call-done, s32[1024]{0:T(1024)S(1)} %broadcast_clamp_fusion.2), kind=kCustom, calls=%fused_computation | custom fusion | bytes 16781312 | tf_op jit(solution)/shard_map/jit(_take)/gather | solution.py:30
  384.5 6.2 select_bitcast_fusion
  390.7 9.3 %copy.10 = f32[2048,1024]{1,0:T(8,128)} copy(f32[2048,1024]{0,1:T(8,128)} %select_bitcast_fusion) | data formatting | bytes 16777216 | tf_op jit(solution)/shard_map/jit(_where)/select_n | solution.py:31
  400.0 15.1 %gather_fusion.1 = f32[2048,1024]{1,0:T(8,128)} fusion(f32[2048,1024]{1,0:T(8,128)} %copy.10, s32[2048]{0:T(1024)S(1)} %broadcast_clamp_fusion), kind=kCustom, calls=%fused_computation.1 | custom fusion | bytes 16785408 | tf_op jit(solution)/shard_map/jit(_take)/gather | solution.py:34
  415.1 5.9 select_select_fusion
  421.0 0.0 reduce-scatter.3.cloned.1.call-update
  421.1 0.0 all-gather.9.cloned.1.call-start
  421.1 0.7 all-gather.9.cloned.1.call-update
  421.8 0.0 all-gather.7.cloned.1.call-start
  421.9 14.4 %reduce-scatter.3.cloned.1.call-done = f32[1024,1024]{1,0:T(8,128)} async-done(((f32[2048,1024]{1,0:T(8,128)}), f32[1024,1024]{1,0:T(8,128)}) %reduce-scatter.3.cloned.1.call-update) | async-done | bytes 4194320 | tf_op jit(solution)/shard_map/reduce_scatter | solution.py:35
  436.2 0.0 all-gather.7.cloned.1.call-update
  436.2 0.0 reduce-scatter.5.cloned.1.call-start
  436.3 1.9 collective-permute-start
  438.2 20.8 %all-gather.9.cloned.1.call-done = f32[1,2048,1024]{2,1,0:T(8,128)} async-done(((f32[1,1024,1024]{2,1,0:T(8,128)}), f32[1,2048,1024]{2,1,0:T(8,128)}) %all-gather.9.cloned.1.call-update) | async-done | bytes 8388624 | tf_op jit(solution)/shard_map/all_gather | solution.py:41
  459.0 160.5 %all-gather.7.cloned.1.call-done = f32[1024,2048]{1,0:T(8,128)} async-done(((f32[1024,1024]{1,0:T(8,128)}), f32[1024,2048]{1,0:T(8,128)}) %all-gather.7.cloned.1.call-update) | async-done | bytes 8388624 | tf_op jit(solution)/shard_map/all_gather | solution.py:38
  619.5 0.0 copy-start
  619.5 29.9 %fusion.6 = f32[1024,1024]{1,0:T(8,128)S(1)} fusion(f32[1024,2048]{1,0:T(8,128)} %all-gather.7.cloned.1.call-done, f32[1,2048,1024]{2,1,0:T(8,128)} %all-gather.9.cloned.1.call-done), kind=kOutput, calls=%fused_computation.9 | convolution fusion | flops 25769803776 | bytes 20971520 | tf_op jit(solution)/shard_map/dot_general | solution.py:39
  649.4 0.0 copy-start.1
  649.4 0.0 collective-permute-done
  649.4 2.0 copy-done.1
  651.4 0.0 copy-done
  651.4 31.0 %fusion.10 = f32[2048,1024]{1,0:T(8,128)} fusion(f32[1024,1024]{1,0:T(8,128)} %collective-permute-done, f32[1024,1024]{1,0:T(8,128)S(1)} %bitcast.28, pred[]{:T(512)S(6)} %eq.3, f32[1024,1024]{1,0:T(8,128)S(1)} %fusion.6), kind=kOutput, calls=%fused_computation.16 | convolution fusion | flops 25779240960 | bytes 20971520 | tf_op jit(solution)/shard_map/dot_general | solution.py:54
  682.4 0.0 reduce-scatter.5.cloned.1.call-update
  682.5 5.0 negate_bitcast_fusion
  687.5 13.1 %reduce-scatter.5.cloned.1.call-done = f32[1024,1024]{1,0:T(8,128)} async-done(((f32[2048,1024]{1,0:T(8,128)}), f32[1024,1024]{1,0:T(8,128)}) %reduce-scatter.5.cloned.1.call-update) | async-done | bytes 4194320 | tf_op jit(solution)/shard_map/reduce_scatter | solution.py:53
  700.6 6.8 fusion.8
  (6 shorter events, 0.1 us)
Async XLA Ops:
  7.2 357.8 %all-gather.5.cloned.1.call-start = ((), (), s32[]{:S(2)}) async-start(), calls=%async_computation.2 | async-start | bytes 35651584 | tf_op jit(solution)/shard_map/all_gather | solution.py:27
  10.1 426.1 %reduce-scatter.3.cloned.1.call-start = ((), (), s32[]{:S(2)}) async-start(), calls=%async_computation.3 | async-start | bytes 12582912 | tf_op jit(solution)/shard_map/reduce_scatter | solution.py:35
  421.1 37.9 %all-gather.9.cloned.1.call-start = ((), (), s32[]{:S(2)}) async-start(), calls=%async_computation.6 | async-start | bytes 12582912 | tf_op jit(solution)/shard_map/all_gather | solution.py:41
  421.8 197.7 %all-gather.7.cloned.1.call-start = ((), (), s32[]{:S(2)}) async-start(), calls=%async_computation.4 | async-start | bytes 12582912 | tf_op jit(solution)/shard_map/all_gather | solution.py:38
  436.2 264.4 %reduce-scatter.5.cloned.1.call-start = ((), (), s32[]{:S(2)}) async-start(), calls=%async_computation.5 | async-start | bytes 12582912 | tf_op jit(solution)/shard_map/reduce_scatter | solution.py:53
  436.3 213.1 %collective-permute-start = (f32[1024,1024]{1,0:T(8,128)}, f32[1024,1024]{1,0:T(8,128)}, u32[]{:S(2)}, u32[]{:S(2)}) collective-permute-start(f32[1024,1024]{1,0:T(8,128)} %bitcast.27), channel_id=1, source_target_pairs={{0,1},{1,0},{2,3},{3,2},{4,5},{5,4},{6,7},{7,6},{8,9},{9,8},{10,11... | collective-permute-start | bytes 12582920 | tf_op jit(solution)/shard_map/ppermute | solution.py:48
  619.5 32.0 %copy-start = (f32[1,1024,1024]{2,1,0:T(8,128)S(1)}, f32[1,1024,1024]{2,1,0:T(8,128)}, u32[]{:S(2)}) copy-start(f32[1,1024,1024]{2,1,0:T(8,128)} %param.6) | copy-start | bytes 12582916
  649.4 2.0 copy-start.1
Sparse Core Ops, SparseCore 0:
  11.3 353.5 all-gather.4
  421.2 14.9 reduce-scatter.2
  437.8 21.1 all-gather.8
  460.5 158.9 all-gather.6
  682.6 17.9 reduce-scatter.4
